TPU v7x, 512 devices: a whole 4x8x8 slice. The times are simulated.
512 devices in a mesh: dp: 32 (over y, x), col: 16 (over z, core).
Axes of the slice: x: 4, y: 8, z: 8, core: 2. Of those that a mesh axis runs over, the one named last changes fastest.
Arguments:
- grad_out: bfloat16 [32768, 3584], P('dp', 'col'), may hold values from -6 to 6
- residual: bfloat16 [32768, 3584], P('dp', 'col'), may hold values from -6 to 6
- confounders: bfloat16 [32768, 512], P('dp'), may hold values from -6 to 6
- gram_factor: float32 [512, 512], replicated, as said below
- proj_weight: bfloat16 [3584, 3584], P('dp', 'col'), may hold values from -0.09375 to 0.09375
- doc_lengths: int32 [32768], P(('dp', 'col')), may hold values from 1 to 512, as said below
Outputs:
- token_grad: float32 [32768, 3584], P(('dp', 'col'))
- weight_grad: float32 [3584, 3584], P('dp', 'col')
Inputs may be any that keep to these rules, and one draw needn't show every extreme that they name: `gram_factor`: lower triangular with a positive diagonal. `doc_lengths`: at least one document has 512 tokens.
All inputs are finite; a program needn't handle non-finite values.
Results may differ from a plain program's by a relative error of at most 0.0026.
Values may be sent and summed in bfloat16 or wider, within the bound.
No kernel may reach another device: no remote copies, remote signals or barrier semaphores. Data moves between devices by JAX's collectives and lax.ppermute only.
A program may use at most 64 MiB of HBM per device.

v0:
```python
import jax
import jax.numpy as jnp
from jax import lax
from jax.sharding import PartitionSpec as P


def solve_gram(factor, rhs):
    inner = lax.linalg.triangular_solve(factor, rhs, left_side=True, lower=True)
    return lax.linalg.triangular_solve(factor, inner, left_side=True, lower=True, transpose_a=True)


def shards(grad_out, residual, confounders, gram_factor, proj_weight, doc_lengths):
    grad_full = lax.all_gather(grad_out, "col", axis=1, tiled=True)
    docs_total = grad_out.shape[0] * lax.axis_size("dp")
    norm_scale = docs_total ** (-0.5)
    own_rows = proj_weight.shape[0]
    full_term = lax.dot_general(
        grad_full, residual, (((0,), (0,)), ((), ())), preferred_element_type=jnp.float32
    )
    summed_all = lax.psum(full_term, "dp")
    summed = lax.dynamic_slice_in_dim(summed_all, lax.axis_index("dp") * own_rows, own_rows, 0)
    weight_grad = summed * norm_scale
    dense_grad = jnp.dot(
        grad_full,
        lax.all_gather(proj_weight, "dp", axis=0, tiled=True),
        preferred_element_type=jnp.float32,
    )
    dense_b = dense_grad.astype(jnp.bfloat16)
    partial_value = lax.dot_general(
        confounders, dense_b, (((0,), (0,)), ((), ())), preferred_element_type=jnp.float32
    )
    moments = lax.psum(partial_value, "dp")
    coef_b = solve_gram(gram_factor, moments).astype(jnp.bfloat16)
    pooled = dense_grad - jnp.dot(confounders, coef_b, preferred_element_type=jnp.float32)
    doc_grad = lax.all_to_all(pooled, "col", split_axis=0, concat_axis=1, tiled=True)
    token_grad = doc_grad / doc_lengths.astype(jnp.float32)[:, None]
    return (token_grad, weight_grad)


def solution(mesh):
    placed = (P("dp", "col"), P("dp", "col"), P("dp", None), P(), P("dp", "col"), P(("dp", "col")))
    return jax.shard_map(
        shards,
        mesh=mesh,
        in_specs=placed,
        out_specs=(P(("dp", "col"), None), P("dp", "col")),
        check_vma=False,
    )
```

profile of v0, /device:TPU:1, one launch (start us, length us, event | category | flops | bytes accessed | tf_op | source)
XLA Modules:
  0.0 392.3 jit_solution(9254413336297546510)
XLA Ops:
  7.2 0.0 all-gather.5.cloned.1.call-start
  7.2 0.7 all-gather.5.cloned.1.call-update
  7.9 0.0 all-gather.3.cloned.1.call-start
  8.0 0.7 all-gather.3.cloned.1.call-update
  8.7 0.0 all-reduce.3.cloned.1.call-start
  8.7 86.1 %all-gather.5.cloned.1.call-done = bf16[3584,224]{1,0:T(8,128)(2,1)} async-done(((bf16[112,224]{1,0:T(8,128)(2,1)}), bf16[3584,224]{1,0:T(8,128)(2,1)}) %all-gather.5.cloned.1.call-update) | async-done | bytes 1605648 | tf_op jit(solution)/shard_map/all_gather | solution.py:25
  94.8 59.2 %all-gather.3.cloned.1.call-done = bf16[1024,3584]{0,1:T(8,128)(2,1)} async-done(((bf16[1024,224]{0,1:T(8,128)(2,1)}), bf16[1024,3584]{0,1:T(8,128)(2,1)}) %all-gather.3.cloned.1.call-update) | async-done | bytes 7340048 | tf_op jit(solution)/shard_map/all_gather | solution.py:13
  154.0 5.6 %fusion.49 = f32[1024,224]{0,1:T(8,128)S(1)} fusion(bf16[1024,3584]{0,1:T(8,128)(2,1)} %all-gather.3.cloned.1.call-done, bf16[3584,224]{1,0:T(8,128)(2,1)} %all-gather.5.cloned.1.call-done), kind=kOutput, calls=%fused_computation.68 | convolution fusion | flops 1644167168 | bytes 9863168 | tf_op jit(solution)/shard_map/dot_general | solution.py:23
  159.6 1.2 convolution_bitcast_fusion.1
  160.8 4.0 %fusion.50 = f32[3584,224]{1,0:T(8,128)} fusion(bf16[1024,3584]{0,1:T(8,128)(2,1)S(1)} %copy-done.1, bf16[1024,224]{0,1:T(8,128)(2,1)S(1)} %copy-done.2), kind=kOutput, calls=%fused_computation.69 | convolution fusion | flops 1644167168 | bytes 11010048 | tf_op jit(solution)/shard_map/dot_general | solution.py:17
  164.8 1.3 fusion.1
  166.2 8.0 %while.1 = (s32[]{:T(128)}, f32[512,512]{1,0:T(8,128)S(1)}, s32[4,2]{0,1:T(2,128)S(1)}, f32[4,128,128]{2,1,0:T(8,128)S(1)}, s32[]{:T(128)}) while((s32[]{:T(128)}, f32[512,512]{1,0:T(8,128)S(1)}, s32[4,2]{0,1:T(2,128)S(1)}, f32[4,128,128]{2,1,0:T(8,128)S(1)}, s32[]{:T(128)}) %tuple.26), condition=%wide.while_cond, body=%wide.while_body.sunk | while | flops 2 | bytes 131189 | solution.py:9
  166.2 0.1 constant_dynamic-slice_fusion.2
  166.3 0.6 fusion.67
  166.9 1.3 bitcast_dynamic-update-slice_fusion.2
  168.2 0.1 constant_dynamic-slice_fusion.2
  168.3 0.6 fusion.67
  168.9 1.3 bitcast_dynamic-update-slice_fusion.2
  170.2 0.1 constant_dynamic-slice_fusion.2
  170.3 0.6 fusion.67
  170.9 1.3 bitcast_dynamic-update-slice_fusion.2
  172.2 0.1 constant_dynamic-slice_fusion.2
  172.3 0.6 fusion.67
  172.9 1.3 bitcast_dynamic-update-slice_fusion.2
  174.2 39.3 %custom-call.5 = f32[4,128,128]{1,2,0:T(8,128)S(1)} custom-call(f32[4,128,128]{2,1,0:T(8,128)S(1)} %get-tuple-element.9), custom_call_target="InvertDiagBlocksLowerTriangular" | custom-call | tf_op jit(solution)/shard_map/triangular_solve | solution.py:9
  213.5 120.8 %all-reduce.3.cloned.1.call-done = (f32[512,224]{0,1:T(8,128)}, f32[3584,224]{1,0:T(8,128)}) async-done(((f32[512,224]{0,1:T(8,128)}, f32[3584,224]{1,0:T(8,128)}), (f32[512,224]{0,1:T(8,128)}, f32[3584,224]{1,0:T(8,128)})) %all-reduce.3.cloned.1.call-update) | async-done | bytes 3670032 | tf_op jit(solution)/shard_map/psum | solution.py:32
  334.3 1.1 fusion.30
  335.5 1.2 convolution_subtract_fusion.1
  336.6 0.2 fusion.35
  336.9 1.3 convolution_subtract_fusion.3
  338.1 0.3 fusion.37
  338.4 1.4 convolution_subtract_fusion.5
  339.8 0.2 fusion.39
  340.0 0.3 fusion.46
  340.3 0.3 convolution_subtract_fusion
  340.5 0.3 fusion.47
  340.8 0.3 convolution_subtract_fusion.2
  341.2 0.3 fusion.48
  341.5 0.5 convolution_subtract_fusion.4
  341.9 0.3 convolution_convert_fusion
  342.2 0.5 fusion
  342.7 1.3 copy.10
  344.0 11.5 %all-to-all-start = ((f32[16,64,224]{2,1,0:T(8,128)}), f32[16,64,224]{2,1,0:T(8,128)S(1)}, u32[]{:S(2)}, u32[]{:S(2)}) async-start(f32[16,64,224]{2,1,0:T(8,128)} %bitcast.6), calls=%async_computation | async-start | bytes 2097152 | tf_op jit(solution)/shard_map/all_to_all | solution.py:35
  355.5 1.6 dynamic-slice_multiply_fusion
  357.1 26.4 %all-to-all-done = f32[16,64,224]{2,1,0:T(8,128)S(1)} async-done(((f32[16,64,224]{2,1,0:T(8,128)}), f32[16,64,224]{2,1,0:T(8,128)S(1)}, u32[]{:S(2)}, u32[]{:S(2)}) %all-to-all-start) | async-done | bytes 917536 | tf_op jit(solution)/shard_map/all_to_all | solution.py:35
  383.5 0.6 copy.11
  384.1 0.6 all_to_all.17
  384.7 1.1 broadcast_divide_fusion
  (13 shorter events, 0.1 us)
Async XLA Ops:
  7.2 152.4 %copy-start = (bf16[1024,512]{1,0:T(8,128)(2,1)S(1)}, bf16[1024,512]{1,0:T(8,128)(2,1)}, u32[]{:S(2)}) copy-start(bf16[1024,512]{1,0:T(8,128)(2,1)} %param.8) | copy-start | bytes 3145732
  7.2 87.6 %all-gather.5.cloned.1.call-start = ((), (), s32[]{:S(2)}) async-start(), calls=%async_computation.2 | async-start | bytes 1892352 | tf_op jit(solution)/shard_map/all_gather | solution.py:25
  7.9 146.0 %all-gather.3.cloned.1.call-start = ((), (), s32[]{:S(2)}) async-start(), calls=%async_computation.1 | async-start | bytes 7798784 | tf_op jit(solution)/shard_map/all_gather | solution.py:13
  8.7 152.1 %copy-start.2 = (bf16[1024,224]{0,1:T(8,128)(2,1)S(1)}, bf16[1024,224]{0,1:T(8,128)(2,1)}, u32[]{:S(2)}) copy-start(bf16[1024,224]{0,1:T(8,128)(2,1)} %param.7) | copy-start | bytes 1376260
  8.7 325.6 %all-reduce.3.cloned.1.call-start = ((), (), s32[]{:S(2)}) async-start(), calls=%async_computation.3 | async-start | bytes 8257536 | tf_op jit(solution)/shard_map/psum | solution.py:32
  154.0 6.8 %copy-start.1 = (bf16[1024,3584]{0,1:T(8,128)(2,1)S(1)}, bf16[1024,3584]{0,1:T(8,128)(2,1)}, u32[]{:S(2)}) copy-start(bf16[1024,3584]{0,1:T(8,128)(2,1)} %all-gather.3.cloned.1.call-done) | copy-start | bytes 22020100
  341.9 13.6 %copy-start.3 = (s32[64]{0:T(128)S(1)}, s32[64]{0:T(128)}, u32[]{:S(2)}) copy-start(s32[64]{0:T(128)} %param.11) | copy-start | bytes 772
  344.0 39.5 %all-to-all-start = ((f32[16,64,224]{2,1,0:T(8,128)}), f32[16,64,224]{2,1,0:T(8,128)S(1)}, u32[]{:S(2)}, u32[]{:S(2)}) async-start(f32[16,64,224]{2,1,0:T(8,128)} %bitcast.6), calls=%async_computation | async-start | bytes 2097152 | tf_op jit(solution)/shard_map/all_to_all | solution.py:35
Sparse Core Ops, SparseCore 0:
  11.1 83.6 all-gather.4
  96.9 57.0 all-gather.2
  164.9 169.3 all-reduce.2
where the time goes:
time: 393 us; the launch traced here: 392 us
  waiting for transfers between devices  294 us (75%)
  other arithmetic  43.3 us (11%)
  matrix products  19.1 us (5%)
  between operations  14 us (4%)
  starting transfers between devices  11.6 us (3%)
  local copies, waits for them, and re-layouts  10.5 us (3%)
    psum x1, waiting for transfers between devices, shards(): moments = lax.psum(partial_value, 'dp')  121 us
    all_gather x1, waiting for transfers between devices, shards(): lax.all_gather(proj_weight, 'dp', axis=0, tiled=True)  86.1 us
    all_gather x1, waiting for transfers between devices, shards(): grad_full = lax.all_gather(grad_out, 'col', axis=1, tiled=True)  59.2 us
    another operation x3, other arithmetic, solve_gram(): lax.linalg.triangular_solve(factor, inner, left_side=True, lower=True, tr...  40.7 us
    all_to_all x1, waiting for transfers between devices, shards(): lax.all_to_all(pooled, 'col', split_axis=0, concat_axis=1, tiled=True)  26.4 us
    all_to_all x1, starting transfers between devices, shards(): lax.all_to_all(pooled, 'col', split_axis=0, concat_axis=1, tiled=True)  11.5 us
    another operation x12, local copies, waits for them, and re-layouts  7.92 us
  transfers between devices with their start and end apart: 4, of which 4 were waited for; matrix products, arithmetic and copies ran while one was open for 13% of the time, Pallas kernels for 0%

commit v1 on v0

--- a/solution.py
+++ b/solution.py
@@ -29,7 +29,23 @@
     partial_value = lax.dot_general(
         confounders, dense_b, (((0,), (0,)), ((), ())), preferred_element_type=jnp.float32
     )
-    moments = lax.psum(partial_value, "dp")
+
+    def balance_outputs(arr_in, chip_axis):
+        cores_n = lax.axis_size(chip_axis)
+
+        def watch_face(next_value, shaped):
+            if shaped >= cores_n:
+                return next_value
+            mixed_arr = lax.ppermute(
+                next_value, axis_name=chip_axis, perm=[(c, c ^ shaped) for c in range(cores_n)]
+            )
+            plain = watch_face(next_value + mixed_arr, 2 * shaped)
+            return plain
+
+        reply = watch_face(arr_in, 1)
+        return reply
+
+    moments = balance_outputs(partial_value, "dp")
     coef_b = solve_gram(gram_factor, moments).astype(jnp.bfloat16)
     pooled = dense_grad - jnp.dot(confounders, coef_b, preferred_element_type=jnp.float32)
     doc_grad = lax.all_to_all(pooled, "col", split_axis=0, concat_axis=1, tiled=True)

time: 393 us -> 450 us (1.15)
  waiting for transfers between devices: 294 us -> 324 us
  starting transfers between devices: 11.6 us -> 29.5 us
  other arithmetic: 43.3 us -> 49.1 us
    ppermute x0 -> x5, waiting for transfers between devices: none -> 35.4 us  [watch_face(): lax.ppermute(next_value, axis_name=chip_axis, perm=[(c, c ^ shaped) for c...]
    all_to_all x1, waiting for transfers between devices: 26.4 us -> 0.01 us  [shards(): lax.all_to_all(pooled, 'col', split_axis=0, concat_axis=1, tiled=True)]
    psum x1, waiting for transfers between devices: 121 us -> 142 us  [shards(): summed_all = lax.psum(full_term, 'dp')]
    ppermute x0 -> x5, starting transfers between devices: none -> 20.1 us  [watch_face(): lax.ppermute(next_value, axis_name=chip_axis, perm=[(c, c ^ shaped) for c...]
  transfers between devices with their start and end apart: 4 -> 9, of which waited for: 4 -> 7; matrix products, arithmetic and copies ran while one was open for 13% -> 15% of each run, Pallas kernels for 0% -> 0%
where the time goes in v1:
time: 450 us; the launch traced here: 447 us
  waiting for transfers between devices  324 us (72%)
  other arithmetic  49.1 us (11%)
  starting transfers between devices  29.5 us (7%)
  matrix products  17.6 us (4%)
  between operations  14 us (3%)
  local copies, waits for them, and re-layouts  12.9 us (3%)
    psum x1, waiting for transfers between devices, shards(): summed_all = lax.psum(full_term, 'dp')  142 us
    all_gather x1, waiting for transfers between devices, shards(): lax.all_gather(proj_weight, 'dp', axis=0, tiled=True)  86.1 us
    all_gather x1, waiting for transfers between devices, shards(): grad_full = lax.all_gather(grad_out, 'col', axis=1, tiled=True)  59.2 us
    another operation x3, other arithmetic, solve_gram(): lax.linalg.triangular_solve(factor, inner, left_side=True, lower=True, tr...  42.1 us
    ppermute x5, waiting for transfers between devices, watch_face(): lax.ppermute(next_value, axis_name=chip_axis, perm=[(c, c ^ shaped) for c...  35.4 us
    ppermute x5, starting transfers between devices, watch_face(): lax.ppermute(next_value, axis_name=chip_axis, perm=[(c, c ^ shaped) for c...  20.1 us
    another operation x12, local copies, waits for them, and re-layouts  10.3 us
    all_to_all x1, starting transfers between devices, shards(): lax.all_to_all(pooled, 'col', split_axis=0, concat_axis=1, tiled=True)  9.27 us
  transfers between devices with their start and end apart: 9, of which 7 were waited for; matrix products, arithmetic and copies ran while one was open for 15% of the time, Pallas kernels for 0%

profile of v1, /device:TPU:1, one launch (start us, length us, event | category | flops | bytes accessed | tf_op | source)
XLA Modules:
  0.0 447.4 jit_solution(7003875107565673772)
XLA Ops:
  7.2 0.7 all-gather.5.cloned.1.call-update
  8.0 0.7 all-gather.3.cloned.1.call-update
  8.7 86.1 %all-gather.5.cloned.1.call-done = bf16[3584,224]{1,0:T(8,128)(2,1)} async-done(((bf16[112,224]{1,0:T(8,128)(2,1)}), bf16[3584,224]{1,0:T(8,128)(2,1)}) %all-gather.5.cloned.1.call-update) | async-done | bytes 1605648 | tf_op jit(solution)/shard_map/all_gather | solution.py:25
  94.8 59.2 %all-gather.3.cloned.1.call-done = bf16[1024,3584]{0,1:T(8,128)(2,1)} async-done(((bf16[1024,224]{0,1:T(8,128)(2,1)}), bf16[1024,3584]{0,1:T(8,128)(2,1)}) %all-gather.3.cloned.1.call-update) | async-done | bytes 7340048 | tf_op jit(solution)/shard_map/all_gather | solution.py:13
  154.0 5.4 %fusion.52 = f32[1024,224]{0,1:T(8,128)S(1)} fusion(bf16[1024,3584]{0,1:T(8,128)(2,1)} %all-gather.3.cloned.1.call-done, bf16[3584,224]{1,0:T(8,128)(2,1)} %all-gather.5.cloned.1.call-done), kind=kOutput, calls=%fused_computation.71 | convolution fusion | flops 1644167168 | bytes 9863168 | tf_op jit(solution)/shard_map/dot_general | solution.py:23
  159.4 0.4 convolution_bitcast_fusion.1
  159.8 3.1 collective-permute-start
  162.9 10.6 %collective-permute-done = f32[512,224]{0,1:T(8,128)S(1)} collective-permute-done((f32[512,224]{0,1:T(8,128)S(1)}, f32[512,224]{0,1:T(8,128)S(1)}, u32[]{:S(2)}, u32[]{:S(2)}) %collective-permute-start) | collective-permute-done | bytes 458784 | tf_op jit(solution)/shard_map/ppermute | solution.py:39
  173.6 4.6 %collective-permute-start.1 = (f32[512,224]{0,1:T(8,128)S(1)}, f32[512,224]{0,1:T(8,128)S(1)}, u32[]{:S(2)}, u32[]{:S(2)}) collective-permute-start(f32[512,224]{0,1:T(8,128)S(1)} %add.24), channel_id=1, source_target_pairs={{0,32},{16,48},{32,0},{48,16},{64,96},{80,112},{96,64},{112,80},{1... | collective-permute-start | bytes 1376264 | tf_op jit(solution)/shard_map/ppermute | solution.py:39
  178.2 9.7 %collective-permute-done.1 = f32[512,224]{0,1:T(8,128)S(1)} collective-permute-done((f32[512,224]{0,1:T(8,128)S(1)}, f32[512,224]{0,1:T(8,128)S(1)}, u32[]{:S(2)}, u32[]{:S(2)}) %collective-permute-start.1) | collective-permute-done | bytes 458784 | tf_op jit(solution)/shard_map/ppermute | solution.py:39
  188.0 3.1 collective-permute-start.2
  191.2 1.3 fusion.1
  192.5 7.6 %collective-permute-done.2 = f32[512,224]{0,1:T(8,128)} collective-permute-done((f32[512,224]{0,1:T(8,128)S(1)}, f32[512,224]{0,1:T(8,128)}, u32[]{:S(2)}, u32[]{:S(2)}) %collective-permute-start.2) | collective-permute-done | bytes 458784 | tf_op jit(solution)/shard_map/ppermute | solution.py:39
  200.1 1.2 add.26
  201.3 4.0 collective-permute-start.3
  205.4 10.4 %while.1 = (s32[]{:T(128)}, f32[512,512]{1,0:T(8,128)S(1)}, s32[4,2]{0,1:T(2,128)S(1)}, f32[4,128,128]{2,1,0:T(8,128)}, s32[]{:T(128)}) while((s32[]{:T(128)}, f32[512,512]{1,0:T(8,128)S(1)}, s32[4,2]{0,1:T(2,128)S(1)}, f32[4,128,128]{2,1,0:T(8,128)}, s32[]{:T(128)}) %tuple.26), condition=%wide.while_cond, body=%wide.while_body.sunk | while | flops 2 | bytes 132205 | solution.py:9
  205.5 0.5 fusion.67
  206.0 2.0 bitcast_dynamic-update-slice_fusion.2
  208.1 0.5 fusion.67
  208.6 2.0 bitcast_dynamic-update-slice_fusion.2
  210.7 0.5 fusion.67
  211.2 2.0 bitcast_dynamic-update-slice_fusion.2
  213.3 0.5 fusion.67
  213.8 2.0 bitcast_dynamic-update-slice_fusion.2
  215.8 40.8 %custom-call.5 = f32[4,128,128]{1,2,0:T(8,128)} custom-call(f32[4,128,128]{2,1,0:T(8,128)} %get-tuple-element.9), custom_call_target="InvertDiagBlocksLowerTriangular" | custom-call | tf_op jit(solution)/shard_map/triangular_solve | solution.py:9
  256.5 1.8 add.27
  258.4 5.3 %collective-permute-start.4 = (f32[512,224]{0,1:T(8,128)}, f32[512,224]{0,1:T(8,128)}, u32[]{:S(2)}, u32[]{:S(2)}) collective-permute-start(f32[512,224]{0,1:T(8,128)} %add.27), channel_id=1, source_target_pairs={{0,256},{16,272},{32,288},{48,304},{64,320},{80,336},{96,352},{112... | collective-permute-start | bytes 1376264 | tf_op jit(solution)/shard_map/ppermute | solution.py:39
  263.7 7.1 %fusion.53 = f32[3584,224]{1,0:T(8,128)} fusion(bf16[1024,3584]{0,1:T(8,128)(2,1)} %all-gather.3.cloned.1.call-done, bf16[1024,224]{0,1:T(8,128)(2,1)} %param.7), kind=kOutput, calls=%fused_computation.72 | convolution fusion | flops 1644167168 | bytes 11010048 | tf_op jit(solution)/shard_map/dot_general | solution.py:17
  270.8 7.5 %collective-permute-done.4 = f32[512,224]{0,1:T(8,128)} collective-permute-done((f32[512,224]{0,1:T(8,128)}, f32[512,224]{0,1:T(8,128)}, u32[]{:S(2)}, u32[]{:S(2)}) %collective-permute-start.4) | collective-permute-done | bytes 458784 | tf_op jit(solution)/shard_map/ppermute | solution.py:39
  278.3 1.2 add.28
  279.8 0.3 fusion.38
  280.3 0.4 fusion.14
  280.9 0.5 fusion.3
  281.7 0.3 fusion.49
  281.9 0.2 convolution_subtract_fusion
  282.2 0.3 fusion.50
  282.5 0.4 convolution_subtract_fusion.1
  282.8 0.3 fusion.51
  283.1 0.5 convolution_subtract_fusion.2
  283.6 0.3 convolution_convert_fusion
  283.8 0.5 fusion
  284.3 1.3 copy.10
  285.6 9.3 %all-to-all-start = ((f32[16,64,224]{2,1,0:T(8,128)}), f32[16,64,224]{2,1,0:T(8,128)S(1)}, u32[]{:S(2)}, u32[]{:S(2)}) async-start(f32[16,64,224]{2,1,0:T(8,128)} %bitcast.6), calls=%async_computation | async-start | bytes 2097152 | tf_op jit(solution)/shard_map/all_to_all | solution.py:51
  294.9 142.1 %all-reduce.2.cloned.1.call-done = f32[3584,224]{1,0:T(8,128)} async-done(((f32[3584,224]{1,0:T(8,128)}), f32[3584,224]{1,0:T(8,128)}) %all-reduce.2.cloned.1.call-update) | async-done | bytes 3211280 | tf_op jit(solution)/shard_map/psum | solution.py:20
  437.0 1.6 dynamic-slice_multiply_fusion
  438.6 0.6 copy.11
  439.2 0.6 all_to_all.17
  439.8 1.1 broadcast_divide_fusion
  (28 shorter events, 1.6 us)
Async XLA Ops:
  7.2 152.3 %copy-start = (bf16[1024,512]{1,0:T(8,128)(2,1)S(1)}, bf16[1024,512]{1,0:T(8,128)(2,1)}, u32[]{:S(2)}) copy-start(bf16[1024,512]{1,0:T(8,128)(2,1)} %param.8) | copy-start | bytes 3145732
  7.2 87.6 %all-gather.5.cloned.1.call-start = ((), (), s32[]{:S(2)}) async-start(), calls=%async_computation.2 | async-start | bytes 1892352 | tf_op jit(solution)/shard_map/all_gather | solution.py:25
  7.9 146.0 %all-gather.3.cloned.1.call-start = ((), (), s32[]{:S(2)}) async-start(), calls=%async_computation.1 | async-start | bytes 7798784 | tf_op jit(solution)/shard_map/all_gather | solution.py:13
  8.7 428.3 %all-reduce.2.cloned.1.call-start = ((), (), s32[]{:S(2)}) async-start(), calls=%async_computation.3 | async-start | bytes 7340032 | tf_op jit(solution)/shard_map/psum | solution.py:20
  159.8 13.7 %collective-permute-start = (f32[512,224]{0,1:T(8,128)S(1)}, f32[512,224]{0,1:T(8,128)S(1)}, u32[]{:S(2)}, u32[]{:S(2)}) collective-permute-start(f32[512,224]{0,1:T(8,128)S(1)} %convolution_bitcast_fusion.1), channel_id=1, source_target_pairs={{0,16},{16,0},{32,48},{48,32},{64,80},{80,64},{96,112},{112,96},{1... | collective-permute-start | bytes 1376264 | tf_op jit(solution)/shard_map/ppermute | solution.py:39
  173.6 14.3 %collective-permute-start.1 = (f32[512,224]{0,1:T(8,128)S(1)}, f32[512,224]{0,1:T(8,128)S(1)}, u32[]{:S(2)}, u32[]{:S(2)}) collective-permute-start(f32[512,224]{0,1:T(8,128)S(1)} %add.24), channel_id=1, source_target_pairs={{0,32},{16,48},{32,0},{48,16},{64,96},{80,112},{96,64},{112,80},{1... | collective-permute-start | bytes 1376264 | tf_op jit(solution)/shard_map/ppermute | solution.py:39
  188.0 4.5 %copy-start.1 = (f32[512,224]{0,1:T(8,128)}, f32[512,224]{0,1:T(8,128)S(1)}, u32[]{:S(2)}) copy-start(f32[512,224]{0,1:T(8,128)S(1)} %add.25) | copy-start | bytes 1376260
  188.0 12.1 %collective-permute-start.2 = (f32[512,224]{0,1:T(8,128)S(1)}, f32[512,224]{0,1:T(8,128)}, u32[]{:S(2)}, u32[]{:S(2)}) collective-permute-start(f32[512,224]{0,1:T(8,128)S(1)} %add.25), channel_id=1, source_target_pairs={{0,64},{16,80},{32,96},{48,112},{64,0},{80,16},{96,32},{112,48},{1... | collective-permute-start | bytes 1376264 | tf_op jit(solution)/shard_map/ppermute | solution.py:39
  201.3 55.2 %collective-permute-start.3 = (f32[512,224]{0,1:T(8,128)S(1)}, f32[512,224]{0,1:T(8,128)}, u32[]{:S(2)}, u32[]{:S(2)}) collective-permute-start(f32[512,224]{0,1:T(8,128)S(1)} %add.26), channel_id=1, source_target_pairs={{0,128},{16,144},{32,160},{48,176},{64,192},{80,208},{96,224},{112... | collective-permute-start | bytes 1376264 | tf_op jit(solution)/shard_map/ppermute | solution.py:39
  258.4 19.9 %collective-permute-start.4 = (f32[512,224]{0,1:T(8,128)}, f32[512,224]{0,1:T(8,128)}, u32[]{:S(2)}, u32[]{:S(2)}) collective-permute-start(f32[512,224]{0,1:T(8,128)} %add.27), channel_id=1, source_target_pairs={{0,256},{16,272},{32,288},{48,304},{64,320},{80,336},{96,352},{112... | collective-permute-start | bytes 1376264 | tf_op jit(solution)/shard_map/ppermute | solution.py:39
  270.8 8.8 %copy-start.2 = (f32[4,128,128]{1,2,0:T(8,128)S(1)}, f32[4,128,128]{1,2,0:T(8,128)}, u32[]{:S(2)}) copy-start(f32[4,128,128]{1,2,0:T(8,128)} %custom-call.5) | copy-start | bytes 786436
  283.6 11.4 %copy-start.3 = (s32[64]{0:T(128)S(1)}, s32[64]{0:T(128)}, u32[]{:S(2)}) copy-start(s32[64]{0:T(128)} %param.11) | copy-start | bytes 772
  285.6 152.9 %all-to-all-start = ((f32[16,64,224]{2,1,0:T(8,128)}), f32[16,64,224]{2,1,0:T(8,128)S(1)}, u32[]{:S(2)}, u32[]{:S(2)}) async-start(f32[16,64,224]{2,1,0:T(8,128)} %bitcast.6), calls=%async_computation | async-start | bytes 2097152 | tf_op jit(solution)/shard_map/all_to_all | solution.py:51
Sparse Core Ops, SparseCore 0:
  11.1 83.6 all-gather.4
  96.9 57.0 all-gather.2
  270.9 166.0 all-reduce.1
